TPU v7x, 128 devices: a whole 4x4x4 slice. The times are simulated.
128 devices in a mesh: sect: 4 (over x), dom: 32 (over z, y, core).
Axes of the slice: x: 4, y: 4, z: 4, core: 2. Of those that a mesh axis runs over, the one named last changes fastest.
Arguments:
- fluid_source: float32 [16384, 32, 128], P(('sect', 'dom')), may hold values from -8 to 8
- coef_ids: int32 [16384, 32, 128], P(('sect', 'dom')), may hold values from 0 to 15
- coef_table: float32 [16], replicated, may hold values from 0.5 to 8
- owner_device: int32 [16384, 1], P(('sect', 'dom')), may hold values from 0 to 127; in each aligned block of 128 rows (0 to 127, 128 to 255, ...) at most 2 rows name the same one
- owner_slot: int32 [16384, 1], P(('sect', 'dom')), may hold values from 0 to 127
- solid_init: float32 [16384, 128], P(('sect', 'dom')), may hold values from -4 to 4
- solid_load: float32 [16384, 128], P(('sect', 'dom')), may hold values from -6 to 6
- compliance: float32 [128, 128], replicated, may hold values from -0.5 to 0.5
Outputs:
- fluid_state: float32 [16384, 32, 128], P(('sect', 'dom'))
- displacement: float32 [16384, 128], P(('sect', 'dom'))
- coupling_norms: float32 [2], replicated
Inputs may be any that keep to these rules, and one draw needn't show every extreme that they name: `owner_device`: among the 128 rows of one device no owner device is named more than 2 times, a bound that some block reaches.
All inputs are finite; a program needn't handle non-finite values.
Results may differ from a plain program's by a relative error of at most 0.0001.
Values sent between devices are 32-bit elements; how exact they have to be, the bound alone decides.
No kernel may reach another device: no remote copies, remote signals or barrier semaphores. Data moves between devices by JAX's collectives and lax.ppermute only.
A program may use at most 64 MiB of HBM per device.

v0:
```python
import jax
import jax.numpy as jnp
from jax import lax
from jax.sharding import PartitionSpec as P

SWEEPS = 3
COUPLE = 2


relax_factor = 0.5


def with_halo(block, sides, width):
    for axis, dim in sides:
        count = lax.axis_size(axis)
        forward = [(i, i + 1) for i in range(count - 1)]
        backward = [(target, source) for source, target in forward]
        low = lax.ppermute(
            lax.slice_in_dim(block, block.shape[dim] - width, None, axis=dim), axis, forward
        )
        high = lax.ppermute(lax.slice_in_dim(block, 0, width, axis=dim), axis, backward)
        block = jnp.concatenate([low, block, high], axis=dim)
    return block


def neighbours(padded):
    center = padded[1:-1]
    total = padded[2:] + padded[:-2]
    wide_y = jnp.pad(center, ((0, 0), (1, 1), (0, 0)))
    total = total + wide_y[:, 2:, :] + wide_y[:, :-2, :]
    wide_z = jnp.pad(center, ((0, 0), (0, 0), (1, 1)))
    total = total + wide_z[:, :, 2:] + wide_z[:, :, :-2]
    return total


def route_requests(buffer):
    return lax.all_to_all(buffer, ("sect", "dom"), split_axis=0, concat_axis=0, tiled=True)


def route_wall(buffer):
    return lax.all_to_all(buffer, ("sect", "dom"), split_axis=0, concat_axis=0, tiled=True)


def route_traction(buffer):
    return lax.all_to_all(buffer, ("sect", "dom"), split_axis=0, concat_axis=0, tiled=True)


def per_device(
    fluid_source, coef_ids, coef_table, owner_device, owner_slot, solid_init, solid_load, compliance
):
    sect_count = lax.axis_size("sect")
    dom_count = lax.axis_size("dom")
    devices = sect_count * dom_count
    fluid_rows = fluid_source.shape[0]
    row_width = fluid_source.shape[2]
    solid_rows = solid_init.shape[0]
    capacity = 2 * fluid_rows // devices
    highest = lax.Precision.HIGHEST
    diagonal = jnp.full(coef_ids.shape, 6.0, jnp.float32)
    for table_index in range(coef_table.shape[0]):
        diagonal = diagonal + jnp.where(coef_ids == table_index, coef_table[table_index], 0.0)
    destination = owner_device[:, 0]
    owner_hits = (destination[:, None] == jnp.arange(devices, dtype=jnp.int32)[None, :]).astype(
        jnp.int32
    )
    earlier = jnp.cumsum(owner_hits, axis=0) - owner_hits
    ranking = jnp.sum(earlier * owner_hits, axis=1)
    position = destination * capacity + ranking
    slot_places = jnp.arange(devices * capacity, dtype=jnp.int32)
    matches = position[None, :] == slot_places[:, None]
    send_slot = jnp.sum(jnp.where(matches, owner_slot[:, 0][None, :] + 1, 0), axis=1) - 1
    placer = matches.astype(jnp.float32)
    got_slot = route_requests(send_slot.reshape(devices, capacity)).reshape(-1)
    picker = (got_slot[:, None] == jnp.arange(solid_rows, dtype=jnp.int32)[None, :]).astype(
        jnp.float32
    )
    fluid_state = jnp.zeros(fluid_source.shape, jnp.float32)
    displacement = solid_init
    norm_list = []
    for iteration in range(COUPLE):
        answer = jnp.dot(picker, displacement, precision=highest)
        returned = route_wall(answer.reshape(devices, capacity, row_width)).reshape(-1, row_width)
        wall_rows = lax.dot_general(placer, returned, (((0,), (0,)), ((), ())), precision=highest)
        source = fluid_source.at[:, 0, :].add(wall_rows)
        for sweep_index in range(SWEEPS):
            padded = with_halo(fluid_state, ((("sect", "dom"), 0),), 1)
            fluid_state = (source + neighbours(padded)) / diagonal
        traction = fluid_state[:, 0, :] - fluid_state[:, 1, :]
        outgoing = jnp.dot(placer, traction, precision=highest).reshape(
            devices, capacity, row_width
        )
        incoming = route_traction(outgoing).reshape(-1, row_width)
        solid_force = (
            lax.dot_general(picker, incoming, (((0,), (0,)), ((), ())), precision=highest)
            + solid_load
        )
        trial_disp = jnp.dot(solid_force, compliance, precision=highest)
        mismatch = trial_disp - displacement
        local_sum = jnp.sum(mismatch * mismatch)
        norm_list.append(jnp.sqrt(lax.psum(local_sum, ("sect", "dom")) + 1e-06))
        displacement = displacement + relax_factor * mismatch
    coupling_norms = jnp.stack(norm_list)
    return (fluid_state, displacement, coupling_norms)


def solution(mesh):
    placed = (
        P(("sect", "dom"), None, None),
        P(("sect", "dom"), None, None),
        P(),
        P(("sect", "dom"), None),
        P(("sect", "dom"), None),
        P(("sect", "dom"), None),
        P(("sect", "dom"), None),
        P(),
    )
    return jax.shard_map(
        per_device,
        mesh=mesh,
        in_specs=placed,
        out_specs=(P(("sect", "dom"), None, None), P(("sect", "dom"), None), P()),
        check_vma=False,
    )
```

profile of v0, /device:TPU:1, one launch (start us, length us, event | category | flops | bytes accessed | tf_op | source)
XLA Modules:
  0.0 319.1 jit_solution(1240787932027532715)
XLA Ops:
  0.6 0.0 copy-start
  0.7 1.6 copy.35
  2.3 0.1 fusion.60
  2.4 0.2 reduce_window_sum.11
  2.6 0.2 select_reduce_fusion.1
  2.8 0.1 select_reduce_fusion
  2.9 0.1 sub.29
  3.1 20.8 %all_to_all.26 = s32[128,1,2]{2,1,0:T(1,128)S(1)} all-to-all(s32[128,1,2]{2,1,0:T(1,128)S(1)} %bitcast.63), channel_id=1, replica_groups=mesh['sect'=4,'dom'=32] {'sect','dom'}, dimensions={0} | all-to-all | bytes 2048 | tf_op jit(solution)/shard_map/all_to_all | solution.py:37
  23.9 0.5 broadcast.140
  24.4 0.8 reduce.7
  25.2 0.1 eq.162
  25.4 0.9 fusion.49
  26.3 4.6 %all-to-all-start.1 = ((f32[128,2,128]{2,1,0:T(2,128)}), f32[128,2,128]{2,1,0:T(2,128)S(1)}, u32[]{:S(2)}, u32[]{:S(2)}) async-start(f32[128,2,128]{2,1,0:T(2,128)} %bitcast.3), calls=%async_computation.1 | async-start | bytes 262144 | tf_op jit(solution)/shard_map/all_to_all | solution.py:41
  30.9 3.0 collective-permute-start
  33.9 2.6 collective-permute-start.1
  36.5 0.1 slice.251
  36.6 1.3 copy.33
  37.9 0.7 fusion.66
  38.6 2.2 all-to-all-done.1
  40.8 0.3 fusion.42
  41.1 3.0 scatter-add.6
  44.1 0.3 broadcast_in_dim.90
  44.4 16.0 %fusion.6 = f32[128,32,128]{2,1,0:T(8,128)S(1)} fusion(f32[128,32,128]{2,1,0:T(8,128)} %scatter-add.6, f32[1,32,128]{2,1,0:T(8,128)S(1)} %collective-permute-done, f32[1,32,128]{2,1,0:T(8,128)S(1)} %collective-permute-done.1, f32[128,32,128]{2,1,0:T(8,128)S(1)} %broadcast_in_dim.90, f32[]{:T(128)} %bitcast.22, s32[128,32,128]{2,1,0:T(8,128)S(1)} %copy-done.1, ...), kind=kLoop, calls=%fused_computation.32 | loop fusion | flops 28835840 | bytes 8421440 | tf_op jit(solution)/shard_map/div | solution.py:87
  60.4 2.4 collective-permute-start.2
  62.9 3.1 collective-permute-start.3
  66.0 0.8 collective-permute-done.3
  66.9 15.3 %fusion.12 = f32[128,32,128]{2,1,0:T(8,128)S(1)} fusion(f32[128,32,128]{2,1,0:T(8,128)S(1)} %copy-done.3, f32[128,32,128]{2,1,0:T(8,128)S(1)} %fusion.6, f32[1,32,128]{2,1,0:T(8,128)S(1)} %collective-permute-done.3, f32[1,32,128]{2,1,0:T(8,128)S(1)} %collective-permute-done.2, f32[]{:T(128)} %bitcast.22, s32[128,32,128]{2,1,0:T(8,128)S(1)} %copy-done.1, ...), kind=kLoop, calls=%fused_computation.38 | loop fusion | flops 29884416 | bytes 8421440 | tf_op jit(solution)/shard_map/div | solution.py:87
  82.2 1.9 collective-permute-start.4
  84.1 4.2 %collective-permute-start.5 = (f32[1,32,128]{2,1,0:T(8,128)S(1)}, f32[1,32,128]{2,1,0:T(8,128)S(1)}, u32[]{:S(2)}, u32[]{:S(2)}) collective-permute-start(f32[1,32,128]{2,1,0:T(8,128)S(1)} %get-tuple-element.36), channel_id=1, source_target_pairs={{0,1},{1,2},{2,3},{3,4},{4,5},{5,6},{6,7},{7,8},{8,9},{9,10},{10,1... | collective-permute-start | bytes 49160 | tf_op jit(solution)/shard_map/ppermute | solution.py:18
  88.3 0.8 collective-permute-done.5
  89.1 15.3 %fusion.18 = f32[128,32,128]{2,1,0:T(8,128)S(1)} fusion(f32[128,32,128]{2,1,0:T(8,128)S(1)} %copy-done.3, f32[128,32,128]{2,1,0:T(8,128)S(1)} %fusion.12, f32[1,32,128]{2,1,0:T(8,128)S(1)} %collective-permute-done.5, f32[1,32,128]{2,1,0:T(8,128)S(1)} %collective-permute-done.4, f32[]{:T(128)} %bitcast.22, s32[128,32,128]{2,1,0:T(8,128)S(1)} %copy-done.1, ...), kind=kLoop, calls=%fused_computation.44 | loop fusion | flops 29884416 | bytes 8421440 | tf_op jit(solution)/shard_map/div | solution.py:87
  104.4 1.3 copy-done.5
  105.8 0.1 slice_subtract_fusion.1
  105.8 0.3 fusion.46
  106.1 0.1 copy.28
  106.2 30.7 %all_to_all.27 = f32[128,2,128]{2,1,0:T(2,128)S(1)} all-to-all(f32[128,2,128]{2,1,0:T(2,128)S(1)} %copy.28), channel_id=1, replica_groups=mesh['sect'=4,'dom'=32] {'sect','dom'}, dimensions={0} | all-to-all | bytes 262144 | tf_op jit(solution)/shard_map/all_to_all | solution.py:45
  136.9 0.4 convolution_add_fusion.1
  137.3 0.2 convolution_subtract_fusion.1
  137.5 0.9 fusion.48
  138.4 4.4 %all-to-all-start.3 = ((f32[128,2,128]{2,1,0:T(2,128)}), f32[128,2,128]{2,1,0:T(2,128)S(1)}, u32[]{:S(2)}, u32[]{:S(2)}) async-start(f32[128,2,128]{2,1,0:T(2,128)} %bitcast.26), calls=%async_computation.3 | async-start | bytes 262144 | tf_op jit(solution)/shard_map/all_to_all | solution.py:41
  142.8 0.7 fusion.63
  143.5 3.0 collective-permute-start.6
  146.5 2.8 collective-permute-start.7
  149.3 3.4 %all-to-all-done.3 = f32[128,2,128]{2,1,0:T(2,128)S(1)} async-done(((f32[128,2,128]{2,1,0:T(2,128)}), f32[128,2,128]{2,1,0:T(2,128)S(1)}, u32[]{:S(2)}, u32[]{:S(2)}) %all-to-all-start.3) | async-done | bytes 131104 | tf_op jit(solution)/shard_map/all_to_all | solution.py:41
  152.7 0.3 fusion.43
  153.0 2.9 scatter-add.9
  156.0 21.3 %fusion.24 = f32[128,32,128]{2,1,0:T(8,128)S(1)} fusion(f32[128,32,128]{2,1,0:T(8,128)} %scatter-add.9, f32[128,32,128]{2,1,0:T(8,128)} %copy-done.5, f32[1,32,128]{2,1,0:T(8,128)S(1)} %collective-permute-done.7, f32[1,32,128]{2,1,0:T(8,128)S(1)} %collective-permute-done.6, f32[]{:T(128)} %bitcast.22, s32[128,32,128]{2,1,0:T(8,128)S(1)} %copy-done.1, ...), kind=kLoop, calls=%fused_computation.50 | loop fusion | flops 29884416 | bytes 8421440 | tf_op jit(solution)/shard_map/div | solution.py:87
  177.3 2.4 collective-permute-start.8
  179.7 3.1 collective-permute-start.9
  182.9 0.8 collective-permute-done.9
  183.7 15.3 %fusion.30 = f32[128,32,128]{2,1,0:T(8,128)S(1)} fusion(f32[128,32,128]{2,1,0:T(8,128)S(1)} %copy-done.4, f32[128,32,128]{2,1,0:T(8,128)S(1)} %fusion.24, f32[1,32,128]{2,1,0:T(8,128)S(1)} %collective-permute-done.9, f32[1,32,128]{2,1,0:T(8,128)S(1)} %collective-permute-done.8, f32[]{:T(128)} %bitcast.22, s32[128,32,128]{2,1,0:T(8,128)S(1)} %copy-done.1, ...), kind=kLoop, calls=%fused_computation.56 | loop fusion | flops 29884416 | bytes 8421440 | tf_op jit(solution)/shard_map/div | solution.py:87
  199.0 1.9 collective-permute-start.10
  200.9 4.2 %collective-permute-start.11 = (f32[1,32,128]{2,1,0:T(8,128)S(1)}, f32[1,32,128]{2,1,0:T(8,128)S(1)}, u32[]{:S(2)}, u32[]{:S(2)}) collective-permute-start(f32[1,32,128]{2,1,0:T(8,128)S(1)} %get-tuple-element.30), channel_id=1, source_target_pairs={{0,1},{1,2},{2,3},{3,4},{4,5},{5,6},{6,7},{7,8},{8,9},{9,10},{10,1... | collective-permute-start | bytes 49160 | tf_op jit(solution)/shard_map/ppermute | solution.py:18
  205.2 0.8 collective-permute-done.11
  206.0 15.3 %fusion.36 = f32[128,32,128]{2,1,0:T(8,128)S(1)} fusion(f32[128,32,128]{2,1,0:T(8,128)S(1)} %copy-done.4, f32[128,32,128]{2,1,0:T(8,128)S(1)} %fusion.30, f32[1,32,128]{2,1,0:T(8,128)S(1)} %collective-permute-done.11, f32[1,32,128]{2,1,0:T(8,128)S(1)} %collective-permute-done.10, f32[]{:T(128)} %bitcast.22, s32[128,32,128]{2,1,0:T(8,128)S(1)} %copy-done.1, ...), kind=kLoop, calls=%fused_computation.62 | loop fusion | flops 29884416 | bytes 8421440 | tf_op jit(solution)/shard_map/div | solution.py:87
  221.3 1.3 copy-done.6
  222.6 0.1 slice_subtract_fusion
  222.7 0.3 fusion.44
  222.9 0.1 copy.30
  223.1 29.4 %all_to_all.28 = f32[128,2,128]{2,1,0:T(2,128)S(1)} all-to-all(f32[128,2,128]{2,1,0:T(2,128)S(1)} %copy.30), channel_id=1, replica_groups=mesh['sect'=4,'dom'=32] {'sect','dom'}, dimensions={0} | all-to-all | bytes 262144 | tf_op jit(solution)/shard_map/all_to_all | solution.py:45
  252.5 0.4 convolution_add_fusion
  252.9 1.5 multiply_reduce_fusion.1
  254.3 62.8 %all-reduce.14 = (f32[]{:T(128)}, f32[]{:T(128)}) all-reduce(f32[]{:T(128)} %get-tuple-element.41, f32[]{:T(128)} %get-tuple-element.39), channel_id=1, replica_groups=mesh['sect'=4,'dom'=32] {'sect','dom'}, use_global_device_ids=true, to_apply=%region_6.7 | all-reduce | flops 2 | bytes 16 | tf_op jit(solution)/shard_map/psum | solution.py:100
  318.5 0.6 pad_maximum_fusion.10
  (38 shorter events, 0.1 us)
Async XLA Ops:
  0.6 136.6 %copy-start = (f32[128,128]{1,0:T(8,128)S(1)}, f32[128,128]{1,0:T(8,128)}, u32[]{:S(2)}) copy-start(f32[128,128]{1,0:T(8,128)} %param.19) | copy-start | bytes 196612
  0.6 1.7 copy-start.10
  0.7 2.1 copy-start.11
  0.7 24.7 %copy-start.7 = (f32[128,128]{1,0:T(8,128)S(1)}, f32[128,128]{1,0:T(8,128)}, u32[]{:S(2)}) copy-start(f32[128,128]{1,0:T(8,128)} %param.17) | copy-start | bytes 196612
  2.3 34.2 %copy-start.2 = (f32[128,32,128]{2,1,0:T(8,128)}, f32[128,32,128]{2,1,0:T(8,128)S(1)}, u32[]{:S(2)}) copy-start(f32[128,32,128]{2,1,0:T(8,128)S(1)} %copy.35) | copy-start | bytes 6291460
  26.3 14.6 %all-to-all-start.1 = ((f32[128,2,128]{2,1,0:T(2,128)}), f32[128,2,128]{2,1,0:T(2,128)S(1)}, u32[]{:S(2)}, u32[]{:S(2)}) async-start(f32[128,2,128]{2,1,0:T(2,128)} %bitcast.3), calls=%async_computation.1 | async-start | bytes 262144 | tf_op jit(solution)/shard_map/all_to_all | solution.py:41
  30.9 13.2 %collective-permute-start = (f32[1,32,128]{2,1,0:T(8,128)S(1)}, f32[1,32,128]{2,1,0:T(8,128)S(1)}, u32[]{:S(2)}, u32[]{:S(2)}) collective-permute-start(f32[1,32,128]{2,1,0:T(8,128)S(1)} %broadcast.126), channel_id=1, source_target_pairs={{1,0},{2,1},{3,2},{4,3},{5,4},{6,5},{7,6},{8,7},{9,8},{10,9},{11,1... | collective-permute-start | bytes 49160 | tf_op jit(solution)/shard_map/ppermute | solution.py:21
  33.9 10.2 %collective-permute-start.1 = (f32[1,32,128]{2,1,0:T(8,128)S(1)}, f32[1,32,128]{2,1,0:T(8,128)S(1)}, u32[]{:S(2)}, u32[]{:S(2)}) collective-permute-start(f32[1,32,128]{2,1,0:T(8,128)S(1)} %broadcast.126), channel_id=1, source_target_pairs={{0,1},{1,2},{2,3},{3,4},{4,5},{5,6},{6,7},{7,8},{8,9},{9,10},{10,1... | collective-permute-start | bytes 49160 | tf_op jit(solution)/shard_map/ppermute | solution.py:18
  36.6 1.3 copy-start.9
  37.9 6.5 %copy-start.1 = (s32[128,32,128]{2,1,0:T(8,128)S(1)}, s32[128,32,128]{2,1,0:T(8,128)}, u32[]{:S(2)}) copy-start(s32[128,32,128]{2,1,0:T(8,128)} %param.13) | copy-start | bytes 6291460
  44.4 22.5 %copy-start.3 = (f32[128,32,128]{2,1,0:T(8,128)S(1)}, f32[128,32,128]{2,1,0:T(8,128)}, u32[]{:S(2)}) copy-start(f32[128,32,128]{2,1,0:T(8,128)} %scatter-add.6) | copy-start | bytes 6291460
  60.4 5.6 %collective-permute-start.2 = (f32[1,32,128]{2,1,0:T(8,128)S(1)}, f32[1,32,128]{2,1,0:T(8,128)S(1)}, u32[]{:S(2)}, u32[]{:S(2)}) collective-permute-start(f32[1,32,128]{2,1,0:T(8,128)S(1)} %get-tuple-element.37), channel_id=1, source_target_pairs={{1,0},{2,1},{3,2},{4,3},{5,4},{6,5},{7,6},{8,7},{9,8},{10,9},{11,1... | collective-permute-start | bytes 49160 | tf_op jit(solution)/shard_map/ppermute | solution.py:21
  62.9 4.0 %collective-permute-start.3 = (f32[1,32,128]{2,1,0:T(8,128)S(1)}, f32[1,32,128]{2,1,0:T(8,128)S(1)}, u32[]{:S(2)}, u32[]{:S(2)}) collective-permute-start(f32[1,32,128]{2,1,0:T(8,128)S(1)} %get-tuple-element.38), channel_id=1, source_target_pairs={{0,1},{1,2},{2,3},{3,4},{4,5},{5,6},{6,7},{7,8},{8,9},{9,10},{10,1... | collective-permute-start | bytes 49160 | tf_op jit(solution)/shard_map/ppermute | solution.py:18
  82.2 6.2 %collective-permute-start.4 = (f32[1,32,128]{2,1,0:T(8,128)S(1)}, f32[1,32,128]{2,1,0:T(8,128)S(1)}, u32[]{:S(2)}, u32[]{:S(2)}) collective-permute-start(f32[1,32,128]{2,1,0:T(8,128)S(1)} %get-tuple-element.35), channel_id=1, source_target_pairs={{1,0},{2,1},{3,2},{4,3},{5,4},{6,5},{7,6},{8,7},{9,8},{10,9},{11,1... | collective-permute-start | bytes 49160 | tf_op jit(solution)/shard_map/ppermute | solution.py:21
  84.1 5.1 %collective-permute-start.5 = (f32[1,32,128]{2,1,0:T(8,128)S(1)}, f32[1,32,128]{2,1,0:T(8,128)S(1)}, u32[]{:S(2)}, u32[]{:S(2)}) collective-permute-start(f32[1,32,128]{2,1,0:T(8,128)S(1)} %get-tuple-element.36), channel_id=1, source_target_pairs={{0,1},{1,2},{2,3},{3,4},{4,5},{5,6},{6,7},{7,8},{8,9},{9,10},{10,1... | collective-permute-start | bytes 49160 | tf_op jit(solution)/shard_map/ppermute | solution.py:18
  88.3 48.6 %copy-start.8 = (f32[128,128]{1,0:T(8,128)S(1)}, f32[128,128]{1,0:T(8,128)}, u32[]{:S(2)}) copy-start(f32[128,128]{1,0:T(8,128)} %param.18) | copy-start | bytes 196612
  104.4 1.3 copy-start.5
  138.4 14.4 %all-to-all-start.3 = ((f32[128,2,128]{2,1,0:T(2,128)}), f32[128,2,128]{2,1,0:T(2,128)S(1)}, u32[]{:S(2)}, u32[]{:S(2)}) async-start(f32[128,2,128]{2,1,0:T(2,128)} %bitcast.26), calls=%async_computation.3 | async-start | bytes 262144 | tf_op jit(solution)/shard_map/all_to_all | solution.py:41
  143.5 12.4 %collective-permute-start.6 = (f32[1,32,128]{2,1,0:T(8,128)S(1)}, f32[1,32,128]{2,1,0:T(8,128)S(1)}, u32[]{:S(2)}, u32[]{:S(2)}) collective-permute-start(f32[1,32,128]{2,1,0:T(8,128)S(1)} %get-tuple-element.33), channel_id=1, source_target_pairs={{1,0},{2,1},{3,2},{4,3},{5,4},{6,5},{7,6},{8,7},{9,8},{10,9},{11,1... | collective-permute-start | bytes 49160 | tf_op jit(solution)/shard_map/ppermute | solution.py:21
  146.5 9.5 %collective-permute-start.7 = (f32[1,32,128]{2,1,0:T(8,128)S(1)}, f32[1,32,128]{2,1,0:T(8,128)S(1)}, u32[]{:S(2)}, u32[]{:S(2)}) collective-permute-start(f32[1,32,128]{2,1,0:T(8,128)S(1)} %get-tuple-element.34), channel_id=1, source_target_pairs={{0,1},{1,2},{2,3},{3,4},{4,5},{5,6},{6,7},{7,8},{8,9},{9,10},{10,1... | collective-permute-start | bytes 49160 | tf_op jit(solution)/shard_map/ppermute | solution.py:18
  156.0 27.8 %copy-start.4 = (f32[128,32,128]{2,1,0:T(8,128)S(1)}, f32[128,32,128]{2,1,0:T(8,128)}, u32[]{:S(2)}) copy-start(f32[128,32,128]{2,1,0:T(8,128)} %scatter-add.9) | copy-start | bytes 6291460
  177.3 5.6 %collective-permute-start.8 = (f32[1,32,128]{2,1,0:T(8,128)S(1)}, f32[1,32,128]{2,1,0:T(8,128)S(1)}, u32[]{:S(2)}, u32[]{:S(2)}) collective-permute-start(f32[1,32,128]{2,1,0:T(8,128)S(1)} %get-tuple-element.31), channel_id=1, source_target_pairs={{1,0},{2,1},{3,2},{4,3},{5,4},{6,5},{7,6},{8,7},{9,8},{10,9},{11,1... | collective-permute-start | bytes 49160 | tf_op jit(solution)/shard_map/ppermute | solution.py:21
  179.7 4.0 %collective-permute-start.9 = (f32[1,32,128]{2,1,0:T(8,128)S(1)}, f32[1,32,128]{2,1,0:T(8,128)S(1)}, u32[]{:S(2)}, u32[]{:S(2)}) collective-permute-start(f32[1,32,128]{2,1,0:T(8,128)S(1)} %get-tuple-element.32), channel_id=1, source_target_pairs={{0,1},{1,2},{2,3},{3,4},{4,5},{5,6},{6,7},{7,8},{8,9},{9,10},{10,1... | collective-permute-start | bytes 49160 | tf_op jit(solution)/shard_map/ppermute | solution.py:18
  199.0 6.1 %collective-permute-start.10 = (f32[1,32,128]{2,1,0:T(8,128)S(1)}, f32[1,32,128]{2,1,0:T(8,128)S(1)}, u32[]{:S(2)}, u32[]{:S(2)}) collective-permute-start(f32[1,32,128]{2,1,0:T(8,128)S(1)} %get-tuple-element.29), channel_id=1, source_target_pairs={{1,0},{2,1},{3,2},{4,3},{5,4},{6,5},{7,6},{8,7},{9,8},{10,9},{11,1... | collective-permute-start | bytes 49160 | tf_op jit(solution)/shard_map/ppermute | solution.py:21
  200.9 5.1 %collective-permute-start.11 = (f32[1,32,128]{2,1,0:T(8,128)S(1)}, f32[1,32,128]{2,1,0:T(8,128)S(1)}, u32[]{:S(2)}, u32[]{:S(2)}) collective-permute-start(f32[1,32,128]{2,1,0:T(8,128)S(1)} %get-tuple-element.30), channel_id=1, source_target_pairs={{0,1},{1,2},{2,3},{3,4},{4,5},{5,6},{6,7},{7,8},{8,9},{9,10},{10,1... | collective-permute-start | bytes 49160 | tf_op jit(solution)/shard_map/ppermute | solution.py:18
  221.3 1.3 copy-start.6
where the time goes:
time: 321 us; the launch traced here: 319 us
  blocking collectives  144 us (45%)
  other arithmetic  101 us (31%)
  starting transfers between devices  43.7 us (14%)
  local copies, waits for them, and re-layouts  14.4 us (4%)
  waiting for transfers between devices  8.99 us (3%)
  matrix products  5.27 us (2%)
    div x6, other arithmetic, per_device(): fluid_state = (source + neighbours(padded)) / diagonal  98.4 us
    psum x1, blocking collectives, per_device(): norm_list.append(jnp.sqrt(lax.psum(local_sum, ('sect', 'dom')) + 1e-06))  62.8 us
    all_to_all x2, blocking collectives, route_traction(): lax.all_to_all(buffer, ('sect', 'dom'), split_axis=0, concat_axis=0, tile...  60.1 us
    all_to_all x1, blocking collectives, route_requests(): lax.all_to_all(buffer, ('sect', 'dom'), split_axis=0, concat_axis=0, tile...  20.8 us
    ppermute x6, starting transfers between devices, with_halo(): lax.ppermute(lax.slice_in_dim(block, block.shape[dim] - width, None, axis...  20 us
    ppermute x6, starting transfers between devices, with_halo(): lax.ppermute(lax.slice_in_dim(block, 0, width, axis=dim), axis, backward)  14.7 us
    all_to_all x2, starting transfers between devices, route_wall(): lax.all_to_all(buffer, ('sect', 'dom'), split_axis=0, concat_axis=0, tile...  9.03 us
  transfers between devices with their start and end apart: 14, of which 6 were waited for; matrix products, arithmetic and copies ran while one was open for 3% of the time, Pallas kernels for 0%

commit v1 on v0

v1 whole, which is shorter than its diff:
```python
import functools

import jax
import jax.numpy as jnp
from jax import lax
from jax.experimental import pallas as pl
from jax.experimental.pallas import tpu as pltpu
from jax.sharding import PartitionSpec as P

AXES = ("sect", "dom")
SWEEPS = 3
COUPLE = 2
RELAX = 0.5
ROWS = 128
FY = 32
ROW = 128
CAP = 2
SLOTS = 6
REACH = 2
PAD = 8
EXT = ROWS + 2 * PAD
HIGHEST = lax.Precision.HIGHEST
F32 = jnp.float32
CHUNKS = 8
NEAR_LIMIT = 24 * 1024 * 1024
FAR_LIMIT = 65_500_000


def shape(*dims):
    return jax.ShapeDtypeStruct(dims, F32)


def iota(dims, axis):
    return lax.broadcasted_iota(jnp.int32, dims, axis)


def kernel_call(
    body, outs, *args, scratch=(), far=(), far_out=(), alias=None, flops=1e6, moved=1e6, name=None
):
    def spec(is_far):
        return pl.BlockSpec(memory_space=pltpu.HBM if is_far else pltpu.VMEM)

    single = not isinstance(outs, tuple)
    out_specs = [spec(k in far_out) for k in range(1 if single else len(outs))]
    return pl.pallas_call(
        body,
        out_shape=outs,
        in_specs=[spec(k in far) for k in range(len(args))],
        out_specs=out_specs[0] if single else out_specs,
        scratch_shapes=list(scratch),
        input_output_aliases=alias or {},
        compiler_params=pltpu.CompilerParams(vmem_limit_bytes=FAR_LIMIT if far else NEAR_LIMIT),
        cost_estimate=pl.CostEstimate(
            flops=int(flops), bytes_accessed=int(moved), transcendentals=0
        ),
        name=name,
    )(*args)


def dot(a, b):
    return jnp.dot(a, b, precision=HIGHEST, preferred_element_type=F32)


def request_body(od_ref, os_ref, req_ref, poscol_ref, posrow_ref):
    sq = (ROWS, ROWS)
    sub, lane = iota(sq, 0).astype(F32), iota(sq, 1).astype(F32)
    od_r, os_r = od_ref[...].astype(F32), os_ref[...].astype(F32)
    od_c = jnp.sum(jnp.where(sub == lane, od_r, 0.0), axis=1, keepdims=True)
    od_c = jnp.broadcast_to(od_c, sq)
    same = od_c == od_r
    rank_c = jnp.sum(jnp.where(same & (lane < sub), 1.0, 0.0), axis=1, keepdims=True)
    rank_r = jnp.sum(jnp.where(same & (sub < lane), 1.0, 0.0), axis=0, keepdims=True)
    edge = jnp.full((PAD, ROW), -1.0, F32)
    poscol_ref[0:PAD] = edge
    poscol_ref[PAD : PAD + ROWS] = od_c * SLOTS + rank_c
    poscol_ref[PAD + ROWS : EXT] = edge
    posrow_ref[...] = jnp.broadcast_to(od_r * CAP + rank_r, (8, ROWS))
    code_r = os_r * ROWS + lane[0:1] + 1.0
    wanted = od_r == sub
    first = jnp.sum(jnp.where(wanted & (rank_r == 0.0), code_r, 0.0), axis=1, keepdims=True)
    second = jnp.sum(jnp.where(wanted & (rank_r == 1.0), code_r, 0.0), axis=1, keepdims=True)
    req_ref[...] = jnp.where(lane == 0.0, first, jnp.where(lane == 1.0, second, 0.0))


def pick_body(devices, recv_ref, disp_ref, ans_ref, sel_ref, slotrow_ref):
    got = recv_ref[...]
    one = got[:, 0:1] - 1.0
    two = got[:, 1:2] - 1.0
    slot_a, slot_b = jnp.floor(one / ROWS), jnp.floor(two / ROWS)
    row_a, row_b = one - slot_a * ROWS, two - slot_b * ROWS
    slot_a, slot_b = slot_a + 1.0, slot_b + 1.0
    lane = iota((devices, ROW), 1)
    beside = jnp.where(
        lane < 4,
        jnp.where(lane == 2, ROWS - 2.0, ROWS - 1.0),
        jnp.where(lane == 4, 0.0, jnp.where(lane == 5, 1.0, -5.0)),
    )
    halo = jnp.where(row_a == beside, slot_a, 0.0) + jnp.where(row_b == beside, slot_b, 0.0)
    table = jnp.where(lane == 0, slot_a, jnp.where(lane == 1, slot_b, halo))
    count = devices * SLOTS
    index = iota((count, devices), 0)
    target = lax.shift_right_logical(index * 10923, 16)
    kind = index - SLOTS * target
    source = target + jnp.where(kind < 2, 0, jnp.where(kind < 4, -1, 1))
    spread = jnp.where(source == iota((count, devices), 1), 1.0, 0.0)
    spread = jnp.dot(
        spread.astype(jnp.bfloat16), table.astype(jnp.bfloat16), preferred_element_type=F32
    )
    index = iota((count, ROW), 0)
    lanes = iota((count, ROW), 1)
    kind = index - SLOTS * lax.shift_right_logical(index * 10923, 16)
    sel = jnp.sum(jnp.where(lanes == kind, spread, 0.0), axis=1, keepdims=True)
    sel_ref[...] = jnp.broadcast_to(sel, (count, ROW))
    ans_ref[...] = dot(jnp.where(sel == lanes.astype(F32) + 1.0, 1.0, 0.0), disp_ref[...])
    wide = (devices, CAP * devices)
    col = iota(wide, 1)
    value = jnp.where((col & 1) == 0, slot_a, slot_b)
    mine = iota(wide, 0) == lax.shift_right_logical(col, 1)
    slotrow = jnp.sum(jnp.where(mine, value, 0.0), axis=0, keepdims=True)
    slotrow_ref[...] = jnp.broadcast_to(slotrow, (8, CAP * devices))


def solid_core(inc_ref, slotrow_ref, disp_ref, load_ref, comp_ref):
    count = inc_ref.shape[0]
    place = jnp.where(
        slotrow_ref[0:1] == iota((ROWS, count), 0).astype(F32) + 1.0, 1.0, 0.0
    )
    force = dot(place, inc_ref[...]) + load_ref[...]
    disp = disp_ref[...]
    mismatch = dot(force, comp_ref[...]) - disp
    square = mismatch * mismatch
    total = jnp.sum(jnp.sum(square, axis=0, keepdims=True), axis=1, keepdims=True)
    return disp, mismatch, total


def solid_body(
    inc_ref, slotrow_ref, disp_ref, load_ref, comp_ref, sel_ref, after_ref, ans_ref, new_ref,
    part_ref,
):
    disp, mismatch, total = solid_core(inc_ref, slotrow_ref, disp_ref, load_ref, comp_ref)
    new = disp + RELAX * mismatch
    new_ref[...] = new
    part_ref[...] = jnp.broadcast_to(total, part_ref.shape)
    sel = sel_ref[...]
    hot = jnp.where(sel == iota(sel.shape, 1).astype(F32) + 1.0, 1.0, 0.0)
    ans_ref[...] = dot(hot, new)


def last_body(
    devices, inc_ref, slotrow_ref, disp_ref, load_ref, comp_ref, part_ref, after_ref, new_ref,
    norm_ref,
):
    disp, mismatch, total = solid_core(inc_ref, slotrow_ref, disp_ref, load_ref, comp_ref)
    new_ref[...] = disp + RELAX * mismatch
    lane = iota((devices, ROW), 1)
    norm_ref[...] = jnp.where(lane == 0, part_ref[0:1], jnp.where(lane == 1, total, 0.0))


def edges_body(fs_ref, ids_ref, up_ref, down_ref, buf_ref, sem):
    edge = REACH * FY
    copies = []
    for k, at in enumerate((ROWS * FY - edge, 0)):
        out = (up_ref, down_ref)[k]
        copies.append(
            pltpu.make_async_copy(fs_ref.at[pl.ds(at, edge)], out.at[pl.ds(0, edge)], sem.at[2 * k])
        )
        copies.append(
            pltpu.make_async_copy(ids_ref.at[pl.ds(at, edge)], buf_ref.at[k], sem.at[2 * k + 1])
        )
    for copy in copies:
        copy.start()
    for copy in copies:
        copy.wait()
    up_ref[edge:] = buf_ref[0].astype(F32) + 1.0
    down_ref[edge:] = buf_ref[1].astype(F32) + 1.0


def prepare_body(
    fs_hbm, ids_hbm, tab_ref, left_ref, right_ref, after_ref, b_hbm, inv_hbm, bt_ref, it_ref,
    fs_ref, ids_ref, b_ref, inv_ref, sem, osem,
):
    step = ROWS // CHUNKS
    loads = []
    for c in range(CHUNKS):
        part = pl.ds(c * step * FY, step * FY)
        pair = (
            pltpu.make_async_copy(fs_hbm.at[part], fs_ref.at[part], sem.at[0, c]),
            pltpu.make_async_copy(ids_hbm.at[part], ids_ref.at[part], sem.at[1, c]),
        )
        for copy in pair:
            copy.start()
        loads.append(pair)
    tab = jnp.broadcast_to(tab_ref[0:1], (FY, ROW))

    def look(ids):
        return jnp.take_along_axis(tab, ids, axis=1, mode="promise_in_bounds")

    for ref, base in ((left_ref, 0), (right_ref, REACH + ROWS)):
        for k in range(REACH):
            marked = ref[(REACH + k) * FY : (REACH + k + 1) * FY, :].astype(jnp.int32)
            inv = look(jnp.maximum(marked - 1, 0))
            inv = jnp.where(marked > 0, inv, 0.0)
            at = (base + k) * FY
            inv_ref[at : at + FY, :] = inv
            b_ref[at : at + FY, :] = inv * ref[k * FY : (k + 1) * FY, :]

    def plane(x, carry):
        here = pl.ds(pl.multiple_of(x * FY, FY), FY)
        there = pl.ds(pl.multiple_of((x + REACH) * FY, FY), FY)
        inv = look(ids_ref[here, :])
        inv_ref[there, :] = inv
        b_ref[there, :] = inv * fs_ref[here, :]
        return carry

    stores = []
    for c in range(CHUNKS):
        for copy in loads[c]:
            copy.wait()
        lax.fori_loop(c * step, (c + 1) * step, plane, 0, unroll=8)
        low = 0 if c == 0 else (c * step + REACH) * FY
        high = ((c + 1) * step + REACH + (REACH if c == CHUNKS - 1 else 0)) * FY
        part = pl.ds(low, high - low)
        for k, (src, dst) in enumerate(((b_ref, b_hbm), (inv_ref, inv_hbm))):
            copy = pltpu.make_async_copy(src.at[part], dst.at[part], osem.at[k, c])
            copy.start()
            stores.append(copy)
    zero = jnp.zeros((PAD, ROW), F32)
    for y in range(SWEEPS + 1):
        for src, dst in ((b_ref, bt_ref), (inv_ref, it_ref)):
            at = y * EXT
            dst[at : at + PAD] = zero
            dst[at + PAD + ROWS : at + EXT] = zero
            dst[at + PAD : at + PAD + ROWS] = src[pl.ds(REACH * FY + y, ROWS, stride=FY), :]
            for k in range(REACH):
                dst[at + PAD - REACH + k : at + PAD - REACH + k + 1] = src[
                    k * FY + y : k * FY + y + 1
                ]
                e = REACH + ROWS + k
                dst[at + PAD + ROWS + k : at + PAD + ROWS + k + 1] = src[
                    e * FY + y : e * FY + y + 1
                ]
    for copy in stores:
        copy.wait()


def wall_rows(recv_ref, poscol_ref):
    count = recv_ref.shape[0]
    wide = (EXT, count)
    slot = iota(wide, 1)
    kind = slot - SLOTS * lax.shift_right_logical(slot * 10923, 16)
    e = iota(wide, 0)
    halo = jnp.where(
        e < PAD,
        jnp.where(e >= PAD - REACH, e - (PAD - REACH) + 2, -1),
        jnp.where((e >= PAD + ROWS) & (e < PAD + ROWS + REACH), e - (PAD + ROWS) + 4, -1),
    )
    pos = poscol_ref[:, 0:1].astype(jnp.int32)
    hot = jnp.where((slot == pos) | (kind == halo), 1.0, 0.0)
    return dot(hot, recv_ref[...])


def along_row(s):
    lane = iota(s.shape, 1)
    last = s.shape[1] - 1
    low = jnp.where(lane == 0, 0.0, pltpu.roll(s, 1, axis=1))
    high = jnp.where(lane == last, 0.0, pltpu.roll(s, last, axis=1))
    return low + high


def thin_sweep(state, b, inv, depth):
    out = []
    for y in range(depth):
        s = state[y]
        total = pltpu.roll(s, EXT - 1, axis=0) + pltpu.roll(s, 1, axis=0)
        total = total + state[y + 1]
        if y > 0:
            total = total + state[y - 1]
        total = total + along_row(s)
        out.append(b[y] + inv[y] * total)
    return out


def send_traction(state, posrow_ref, tout_ref):
    traction = (state[0] - state[1])[PAD : PAD + ROWS]
    place = jnp.where(
        posrow_ref[0:1] == iota((tout_ref.shape[0], ROWS), 0).astype(F32), 1.0, 0.0
    )
    tout_ref[...] = dot(place, traction)


def thin_source(recv_ref, poscol_ref, bt_ref, it_ref, w_ref):
    w = wall_rows(recv_ref, poscol_ref)
    w_ref[...] = w
    inv = [it_ref[y * EXT : (y + 1) * EXT, :] for y in range(SWEEPS + 1)]
    b = [bt_ref[y * EXT : (y + 1) * EXT, :] for y in range(SWEEPS + 1)]
    b[0] = b[0] + w * inv[0]
    return b, inv


def thin_first_body(recv_ref, poscol_ref, posrow_ref, bt_ref, it_ref, tout_ref, w_ref):
    b, inv = thin_source(recv_ref, poscol_ref, bt_ref, it_ref, w_ref)
    state = thin_sweep(b, b, inv, 3)
    state = thin_sweep(state, b, inv, 2)
    send_traction(state, posrow_ref, tout_ref)


def thin_next_body(
    recv_ref, poscol_ref, posrow_ref, bt_ref, it_ref, st_ref, left_ref, right_ref, tout_ref,
    w_ref, ext_ref,
):
    zero = jnp.zeros((PAD, ROW), F32)
    for y in range(SWEEPS + 2):
        at = y * EXT
        ext_ref[at : at + PAD] = zero
        ext_ref[at + PAD + ROWS : at + EXT] = zero
        ext_ref[at + PAD : at + PAD + ROWS] = st_ref[y * ROWS : (y + 1) * ROWS]
        for k in range(SWEEPS):
            ext_ref[at + PAD - SWEEPS + k : at + PAD - SWEEPS + k + 1] = left_ref[
                k * FY + y : k * FY + y + 1
            ]
            ext_ref[at + PAD + ROWS + k : at + PAD + ROWS + k + 1] = right_ref[
                k * FY + y : k * FY + y + 1
            ]
    b, inv = thin_source(recv_ref, poscol_ref, bt_ref, it_ref, w_ref)
    state = [ext_ref[y * EXT : (y + 1) * EXT, :] for y in range(SWEEPS + 2)]
    state = thin_sweep(state, b, inv, 4)
    state = thin_sweep(state, b, inv, 3)
    state = thin_sweep(state, b, inv, 2)
    send_traction(state, posrow_ref, tout_ref)


def sweep(src_ref, shift, dst_ref, drop, b_ref, inv_ref, tri_ref, low, count, group):
    sub = iota((8, ROW), 0)

    def planes(g, carry):
        e = low + g * group
        base = pl.multiple_of(e * FY, FY)
        from_ = pl.multiple_of((e + shift) * FY, FY)
        to = pl.multiple_of((e - drop) * FY, FY)
        block = src_ref[pl.ds(from_, group * FY), :]
        coarse = block.astype(jnp.bfloat16)
        fine = (block - coarse.astype(F32)).astype(jnp.bfloat16)
        tri = tri_ref[...]
        along = jnp.dot(coarse, tri, preferred_element_type=F32)
        along = along + jnp.dot(fine, tri, preferred_element_type=F32)
        done = []
        for k in range(0, group * FY, 8):
            at = from_ + k
            total = src_ref[pl.ds(at - FY, 8), :] + src_ref[pl.ds(at + FY, 8), :]
            up, down = src_ref[pl.ds(at - 1, 8), :], src_ref[pl.ds(at + 1, 8), :]
            if k % FY == 0:
                up = jnp.where(sub == 0, 0.0, up)
            if k % FY == FY - 8:
                down = jnp.where(sub == 7, 0.0, down)
            total = total + (up + down)
            total = total + along[k : k + 8]
            done.append(b_ref[pl.ds(base + k, 8), :] + inv_ref[pl.ds(base + k, 8), :] * total)
        for k, value in enumerate(done):
            dst_ref[pl.ds(to + 8 * k, 8), :] = value
        return carry

    lax.fori_loop(0, count // group, planes, 0)


def fetch(pairs, sem):
    copies = [
        pltpu.make_async_copy(src, dst, sem.at[k]) for k, (src, dst) in enumerate(pairs)
    ]
    for copy in copies:
        copy.start()
    return copies


def halves(low, count):
    cut = count // 2
    return pl.ds(low * FY, cut * FY), pl.ds((low + cut) * FY, (count - cut) * FY)


def add_wall(b_ref, inv_ref, w_ref, first, planes):
    top = pl.ds(0, planes, stride=FY)
    b_ref[top, :] = b_ref[top, :] + inv_ref[top, :] * w_ref[first : first + planes, :]


def full_first_body(
    b_hbm, inv_hbm, w_ref, tri_ref, state_hbm, el_ref, er_ref, st_ref, tick_ref, b_ref, inv_ref,
    two_ref, out_ref, sem, osem,
):
    planes = ROWS + 2 * REACH
    pairs = []
    for part in halves(0, planes):
        pairs += [(b_hbm.at[part], b_ref.at[part]), (inv_hbm.at[part], inv_ref.at[part])]
    for copy in fetch(pairs, sem):
        copy.wait()
    add_wall(b_ref, inv_ref, w_ref, PAD - REACH, planes)
    sweep(b_ref, 0, two_ref, 0, b_ref, inv_ref, tri_ref, 1, ROWS + 2, 13)
    sweep(two_ref, 0, out_ref, REACH, b_ref, inv_ref, tri_ref, REACH, ROWS, 16)
    store = fetch([(out_ref.at[part], state_hbm.at[part]) for part in halves(0, ROWS)], osem)
    tick_ref[...] = jnp.zeros_like(tick_ref)
    el_ref[...] = out_ref[0 : SWEEPS * FY]
    er_ref[...] = out_ref[(ROWS - SWEEPS) * FY :]
    for y in range(SWEEPS + 2):
        st_ref[y * ROWS : (y + 1) * ROWS] = out_ref[pl.ds(y, ROWS, stride=FY), :]
    for copy in store:
        copy.wait()


def full_next_body(
    half, b_hbm, inv_hbm, w_ref, tri_ref, s_hbm, left_ref, right_ref, after_ref, out_hbm, tick_ref,
    b_ref, inv_ref, s_ref, two_ref, sem, osem,
):
    own = ROWS // 2
    first = half * own
    pairs = []
    planes = own + 2 * REACH
    for src, dst in zip(halves(first, planes), halves(0, planes)):
        pairs += [(b_hbm.at[src], b_ref.at[dst]), (inv_hbm.at[src], inv_ref.at[dst])]
    planes = own + SWEEPS
    low = max(first - SWEEPS, 0)
    at = SWEEPS if half == 0 else 0
    for src, dst in zip(halves(low, planes), halves(at, planes)):
        pairs.append((s_hbm.at[src], s_ref.at[dst]))
    copies = fetch(pairs, sem)
    if half == 0:
        s_ref[0 : SWEEPS * FY] = left_ref[...]
    else:
        s_ref[(own + SWEEPS) * FY : (own + 2 * SWEEPS) * FY] = right_ref[...]
    for copy in copies:
        copy.wait()
    add_wall(b_ref, inv_ref, w_ref, PAD - REACH + first, own + 2 * REACH)
    sweep(s_ref, 1, two_ref, 0, b_ref, inv_ref, tri_ref, 0, own + 4, 17)
    sweep(two_ref, 0, s_ref, 0, b_ref, inv_ref, tri_ref, 1, own + 2, 11)
    sweep(s_ref, 0, two_ref, REACH, b_ref, inv_ref, tri_ref, REACH, own, 16)
    pairs = []
    for src, dst in zip(halves(0, own), halves(first, own)):
        pairs.append((two_ref.at[src], out_hbm.at[dst]))
    store = fetch(pairs, osem)
    tick_ref[...] = jnp.zeros_like(tick_ref)
    for copy in store:
        copy.wait()


def full_second_body(
    b_hbm, inv_hbm, w_ref, tri_ref, s_hbm, left_ref, right_ref, after_ref, begun_hbm, *rest
):
    full_next_body(
        1, b_hbm, inv_hbm, w_ref, tri_ref, s_hbm, left_ref, right_ref, after_ref, *rest
    )


def exchange(buffer, devices):
    width = buffer.size // devices
    rows = buffer.reshape(devices, 1, width) if width != CAP * ROW else buffer.reshape(
        devices, CAP, ROW
    )
    got = lax.all_to_all(rows, AXES, split_axis=0, concat_axis=0, tiled=True)
    return got.reshape(buffer.shape)


def beside(to_right, to_left, devices):
    up = [(i, i + 1) for i in range(devices - 1)]
    down = [(i + 1, i) for i in range(devices - 1)]
    return lax.ppermute(to_right, AXES, up), lax.ppermute(to_left, AXES, down)


def buffers(*planes):
    return tuple(pltpu.VMEM((count * FY, ROW), F32) for count in planes)


def per_device(
    devices, fluid_source, coef_ids, coef_table, owner_device, owner_slot, solid_init, solid_load,
    compliance,
):
    fluid = fluid_source.reshape(ROWS * FY, ROW)
    ids = coef_ids.reshape(ROWS * FY, ROW)
    inverse = jnp.pad(1.0 / (6.0 + coef_table), (0, ROW - coef_table.shape[0]))
    inverse = jnp.broadcast_to(inverse[None, :], (8, ROW))
    tri = (jnp.eye(ROW, k=1) + jnp.eye(ROW, k=-1)).astype(jnp.bfloat16)
    edge = 2 * REACH
    dma = pltpu.SemaphoreType.DMA

    req, poscol, posrow = kernel_call(
        request_body, (shape(devices, ROW), shape(EXT, ROW), shape(8, ROWS)),
        owner_device.reshape(1, ROWS), owner_slot.reshape(1, ROWS), name="request",
    )
    wanted = exchange(req, devices)
    up, down = kernel_call(
        edges_body, (shape(edge * FY, ROW), shape(edge * FY, ROW)), fluid, ids, far=(0, 1),
        scratch=(pltpu.VMEM((2, REACH * FY, ROW), jnp.int32), dma((4,))), name="edges",
    )
    left, right = beside(up, down, devices)
    count = devices * SLOTS
    ans, sel, slotrow = kernel_call(
        functools.partial(pick_body, devices),
        (shape(count, ROW), shape(count, ROW), shape(8, CAP * devices)),
        wanted, solid_init, name="pick",
    )
    recv = exchange(ans, devices)
    wide = ROWS + 2 * REACH
    b, inv, bt, it = kernel_call(
        prepare_body,
        (shape(wide * FY, ROW), shape(wide * FY, ROW), shape(4 * EXT, ROW), shape(4 * EXT, ROW)),
        fluid, ids, inverse, left, right, slotrow, far=(0, 1), far_out=(0, 1),
        scratch=(
            *buffers(ROWS), pltpu.VMEM((ROWS * FY, ROW), jnp.int32), *buffers(wide, wide),
            dma((2, CHUNKS)), dma((2, CHUNKS)),
        ),
        flops=1e9, moved=1e7, name="prepare",
    )
    tout, w = kernel_call(
        thin_first_body, (shape(CAP * devices, ROW), shape(EXT, ROW)),
        recv, poscol, posrow, bt, it, name="thin0",
    )
    incoming = exchange(tout, devices)
    state, to_left, to_right, st, tick = kernel_call(
        full_first_body,
        (
            shape(ROWS * FY, ROW), shape(SWEEPS * FY, ROW), shape(SWEEPS * FY, ROW),
            shape((SWEEPS + 2) * ROWS, ROW), shape(8, ROW),
        ),
        b, inv, w, tri, far=(0, 1), far_out=(0,),
        scratch=(*buffers(wide, wide, wide, ROWS), dma((4,)), dma((2,))),
        flops=4e9, moved=1e7, name="full0",
    )
    ans, disp, part = kernel_call(
        solid_body, (shape(count, ROW), shape(ROWS, ROW), shape(8, ROW)),
        incoming, slotrow, solid_init, solid_load, compliance, sel, tick, name="solid0",
    )
    recv = exchange(ans, devices)
    left, right = beside(to_right, to_left, devices)
    tout, w = kernel_call(
        thin_next_body, (shape(CAP * devices, ROW), shape(EXT, ROW)),
        recv, poscol, posrow, bt, it, st, left, right,
        scratch=(pltpu.VMEM(((SWEEPS + 2) * EXT, ROW), F32),), name="thin1",
    )
    incoming = exchange(tout, devices)
    own = ROWS // 2
    scratch = (
        *buffers(own + 2 * REACH, own + 2 * REACH, own + 2 * SWEEPS, own + 2 * REACH),
        dma((6,)), dma((2,)),
    )
    begun, tick = kernel_call(
        functools.partial(full_next_body, 0), (shape(ROWS * FY, ROW), shape(8, ROW)),
        b, inv, w, tri, state, left, right, posrow, far=(0, 1, 4), far_out=(0,), scratch=scratch,
        flops=4e9, moved=1e7, name="full1",
    )
    disp, norm = kernel_call(
        functools.partial(last_body, devices), (shape(ROWS, ROW), shape(devices, ROW)),
        incoming, slotrow, disp, solid_load, compliance, part, tick, name="solid1",
    )
    norms = exchange(norm, devices)
    state, _ = kernel_call(
        full_second_body, (shape(ROWS * FY, ROW), shape(8, ROW)),
        b, inv, w, tri, state, left, right, disp, begun, far=(0, 1, 4, 8), far_out=(0,),
        alias={8: 0}, scratch=scratch, flops=4e9, moved=1e7, name="full2",
    )
    norms = jnp.sqrt(jnp.sum(norms[:, :COUPLE], axis=0) + 1e-06)
    return state.reshape(ROWS, FY, ROW), disp, norms


def solution(mesh):
    devices = mesh.shape["sect"] * mesh.shape["dom"]
    rows, planes = P(AXES, None), P(AXES, None, None)
    return jax.shard_map(
        functools.partial(per_device, devices),
        mesh=mesh,
        in_specs=(planes, planes, P(), rows, rows, rows, rows, P()),
        out_specs=(planes, rows, P()),
        check_vma=False,
    )
```

time: 321 us -> 135 us (0.42)
  blocking collectives: 144 us -> 0 us
  other arithmetic: 101 us -> 1.27 us
  Pallas kernels: 0 us -> 41.7 us
  waiting for transfers between devices: 8.99 us -> 25.1 us
  starting transfers between devices: 43.7 us -> 58.6 us
  local copies, waits for them, and re-layouts: 14.4 us -> 6.77 us
  matrix products: 5.27 us -> 0 us
    div x6 -> x1, other arithmetic: 98.4 us -> 0.01 us  [per_device(): inverse = jnp.pad(1.0 / (6.0 + coef_table), (0, ROW - coef_table.shape[0]))]
    all_to_all x3 -> x0, blocking collectives: 80.9 us -> none  [the longest x2 60.1 us: route_traction(): lax.all_to_all(buffer, ('sect', 'dom'), split_axis=0, concat_axis=0, tile...]
    psum x1 -> x0, blocking collectives: 62.8 us -> none  [per_device(): norm_list.append(jnp.sqrt(lax.psum(local_sum, ('sect', 'dom')) + 1e-06))]
    pallas_call x0 -> x11, Pallas kernels: none -> 41.7 us  [kernel_call(): pl.pallas_call(body, out_shape=outs, in_specs=[spec(k in far) for k in ra...]
    all_to_all x2 -> x6, starting transfers between devices: 9.03 us -> 46.6 us  [exchange(): got = lax.all_to_all(rows, AXES, split_axis=0, concat_axis=0, tiled=True)]
    ppermute x12 -> x4, starting transfers between devices: 34.7 us -> 12 us  [beside(): return (lax.ppermute(to_right, AXES, up), lax.ppermute(to_left, AXES, down))]
    all_to_all x2 -> x6, waiting for transfers between devices: 5.64 us -> 21.1 us  [exchange(): got = lax.all_to_all(rows, AXES, split_axis=0, concat_axis=0, tiled=True)]
    scatter-add x2 -> x0, local copies, waits for them, and re-layouts: 5.9 us -> none  [per_device(): source = fluid_source.at[:, 0, :].add(wall_rows)]
  transfers between devices with their start and end apart: 14 -> 10, of which waited for: 6 -> 8; matrix products, arithmetic and copies ran while one was open for 3% -> 1% of each run, Pallas kernels for 0% -> 25%
where the time goes in v1:
time: 135 us; the launch traced here: 134 us
  starting transfers between devices  58.6 us (43%)
  Pallas kernels  41.7 us (31%)
  waiting for transfers between devices  25.1 us (19%)
  local copies, waits for them, and re-layouts  6.77 us (5%)
    all_to_all x6, starting transfers between devices, exchange(): got = lax.all_to_all(rows, AXES, split_axis=0, concat_axis=0, tiled=True)  46.6 us
    pallas_call x11, Pallas kernels, kernel_call(): pl.pallas_call(body, out_shape=outs, in_specs=[spec(k in far) for k in ra...  41.7 us
    all_to_all x6, waiting for transfers between devices, exchange(): got = lax.all_to_all(rows, AXES, split_axis=0, concat_axis=0, tiled=True)  21.1 us
    ppermute x4, starting transfers between devices, beside(): return (lax.ppermute(to_right, AXES, up), lax.ppermute(to_left, AXES, down))  12 us
    unnamed x44, local copies, waits for them, and re-layouts  6.17 us
    ppermute x4, waiting for transfers between devices, beside(): return (lax.ppermute(to_right, AXES, up), lax.ppermute(to_left, AXES, down))  3.99 us
  transfers between devices with their start and end apart: 10, of which 8 were waited for; matrix products, arithmetic and copies ran while one was open for 1% of the time, Pallas kernels for 25%

profile of v1, /device:TPU:1, one launch (start us, length us, event | category | flops | bytes accessed | tf_op | source)
XLA Modules:
  0.0 134.3 jit_solution(17053232358584091271)
XLA Ops:
  0.6 0.0 copy-start.17
  0.6 0.0 copy-start.18
  0.7 0.0 copy-start.5
  0.7 0.0 copy-start.21
  0.7 1.5 %edges.1 = (f32[128,128]{1,0:T(8,128)}, f32[128,128]{1,0:T(8,128)}) custom-call(f32[4096,128]{1,0:T(8,128)} %bitcast.28, s32[4096,128]{1,0:T(8,128)} %bitcast.30), custom_call_target="tpu_custom_call" | custom-call | flops 1000000 | bytes 1000000 | tf_op jit(solution)/shard_map/edges/pallas_call | solution.py:45
  2.2 4.6 %collective-permute-start = (f32[128,128]{1,0:T(8,128)}, f32[128,128]{1,0:T(8,128)S(1)}, u32[]{:S(2)}, u32[]{:S(2)}) collective-permute-start(f32[128,128]{1,0:T(8,128)} %get-tuple-element.32), channel_id=1, source_target_pairs={{0,1},{1,2},{2,3},{3,4},{4,5},{5,6},{6,7},{7,8},{8,9},{9,10},{10,1... | collective-permute-start | bytes 196616 | tf_op jit(solution)/shard_map/ppermute | solution.py:462
  6.8 1.9 %collective-permute-start.1 = (f32[128,128]{1,0:T(8,128)}, f32[128,128]{1,0:T(8,128)S(1)}, u32[]{:S(2)}, u32[]{:S(2)}) collective-permute-start(f32[128,128]{1,0:T(8,128)} %get-tuple-element.33), channel_id=1, source_target_pairs={{1,0},{2,1},{3,2},{4,3},{5,4},{6,5},{7,6},{8,7},{9,8},{10,9},{11,1... | collective-permute-start | bytes 196616 | tf_op jit(solution)/shard_map/ppermute | solution.py:462
  8.7 0.0 copy-done.17
  8.7 0.0 copy-done.18
  8.7 0.8 request.1
  9.6 10.5 %all-to-all-start = ((f32[128,1,128]{2,1,0:T(1,128)}), f32[128,1,128]{2,1,0:T(1,128)S(1)}, u32[]{:S(2)}, u32[]{:S(2)}) async-start(f32[128,1,128]{2,1,0:T(1,128)} %bitcast.5), calls=%async_computation | async-start | bytes 131072 | tf_op jit(solution)/shard_map/all_to_all | solution.py:455
  20.1 9.4 %all-to-all-done = f32[128,1,128]{2,1,0:T(1,128)S(1)} async-done(((f32[128,1,128]{2,1,0:T(1,128)}), f32[128,1,128]{2,1,0:T(1,128)S(1)}, u32[]{:S(2)}, u32[]{:S(2)}) %all-to-all-start) | async-done | bytes 65568 | tf_op jit(solution)/shard_map/all_to_all | solution.py:455
  29.6 0.0 copy-done.5
  29.6 1.7 %pick.1 = (f32[768,128]{1,0:T(8,128)}, f32[768,128]{1,0:T(8,128)S(1)}, f32[8,256]{1,0:T(8,128)S(1)}) custom-call(f32[128,128]{1,0:T(8,128)S(1)} %bitcast.25, f32[128,128]{1,0:T(8,128)S(1)} %copy-done.5), custom_call_target="tpu_custom_call" | custom-call | flops 1000000 | bytes 1000000 | tf_op jit(solution)/shard_map/pick/pallas_call | solution.py:45
  31.3 0.6 copy-done.8
  31.8 4.6 %all-to-all-start.1 = ((f32[128,1,768]{2,1,0:T(1,128)}), f32[128,1,768]{2,1,0:T(1,128)S(1)}, u32[]{:S(2)}, u32[]{:S(2)}) async-start(f32[128,1,768]{2,1,0:T(1,128)} %bitcast.7), calls=%async_computation.1 | async-start | bytes 786432 | tf_op jit(solution)/shard_map/all_to_all | solution.py:455
  36.5 0.7 add_convert_fusion.tri_ref
  37.2 0.0 copy-done.21
  37.2 0.0 collective-permute-done.left_ref
  37.2 0.0 copy-start.19
  37.2 0.0 collective-permute-done.1.right_ref
  37.2 0.0 copy-start.20
  37.2 0.6 broadcast_in_dim.2.tab_ref
  37.8 0.0 copy-done.19
  37.8 0.0 copy-done.20
  37.8 6.4 %prepare.1 = (f32[4224,128]{1,0:T(8,128)}, f32[4224,128]{1,0:T(8,128)}, f32[576,128]{1,0:T(8,128)}, f32[576,128]{1,0:T(8,128)}) custom-call(f32[4096,128]{1,0:T(8,128)} %bitcast.29, s32[4096,128]{1,0:T(8,128)} %bitcast.31, f32[8,128]{1,0:T(8,128)} %broadcast_in_dim.2.tab_ref, f32[128,128]{1,0:T(8,128)} %copy-done.19, f32[128,128]{1,0:T(8,128)} %copy-done.20, ...), custom_call_target="tpu_custom_call" | custom-call | flops 1000000000 | bytes 10000000 | tf_op jit(solution)/shard_map/prepare/pallas_call | solution.py:45
  44.3 4.3 %all-to-all-done.1 = f32[128,1,768]{2,1,0:T(1,128)S(1)} async-done(((f32[128,1,768]{2,1,0:T(1,128)}), f32[128,1,768]{2,1,0:T(1,128)S(1)}, u32[]{:S(2)}, u32[]{:S(2)}) %all-to-all-start.1) | async-done | bytes 393248 | tf_op jit(solution)/shard_map/all_to_all | solution.py:455
  48.5 1.0 copy-done
  49.5 1.0 copy-done.2
  50.5 1.9 %thin0.1 = (f32[256,128]{1,0:T(8,128)}, f32[144,128]{1,0:T(8,128)S(1)}) custom-call(f32[768,128]{1,0:T(8,128)S(1)} %bitcast.21, f32[144,128]{1,0:T(8,128)S(1)} %get-tuple-element.39.poscol_ref, f32[8,128]{1,0:T(8,128)S(1)} %get-tuple-element.40.posrow_ref.after_ref, f32[576,128]{1,0:T(8,128)S(1)} %copy-done, f32[576,128]{1,0:T(8,128)S(1)} %copy-done.2), custom_call_target="tpu_custom_call" | custom-call | flops 1000000 | bytes 1000000 | tf_op jit(solution)/shard_map/thin0/pallas_call | solution.py:45
  52.3 0.6 copy-done.16
  53.0 5.5 %all-to-all-start.2 = ((f32[128,2,128]{2,1,0:T(2,128)}), f32[128,2,128]{2,1,0:T(2,128)S(1)}, u32[]{:S(2)}, u32[]{:S(2)}) async-start(f32[128,2,128]{2,1,0:T(2,128)} %bitcast.9), calls=%async_computation.2 | async-start | bytes 262144 | tf_op jit(solution)/shard_map/all_to_all | solution.py:455
  58.5 0.0 copy-start.6
  58.5 0.0 copy-start.7
  58.5 0.0 copy-start.9
  58.5 0.0 copy-start.1
  58.5 0.0 copy-start.3
  58.5 9.4 %full0.1 = (f32[4096,128]{1,0:T(8,128)}, f32[96,128]{1,0:T(8,128)}, f32[96,128]{1,0:T(8,128)}, f32[640,128]{1,0:T(8,128)}, f32[8,128]{1,0:T(8,128)}) custom-call(f32[4224,128]{1,0:T(8,128)} %get-tuple-element.36.b_hbm, f32[4224,128]{1,0:T(8,128)} %get-tuple-element.37.inv_hbm, f32[144,128]{1,0:T(8,128)} %copy-done.16, bf16[128,128]{1,0:T(8,128)(2,1)} %add_convert_fusion.tri_ref), custom_call_target="tpu_custom_call" | custom-call | flops 4000000000 | bytes 10000000 | tf_op jit(solution)/shard_map/full0/pallas_call | solution.py:45
  68.0 0.5 all-to-all-done.2
  68.4 0.0 copy-done.6
  68.4 0.0 copy-start.13
  68.5 0.7 copy-done.13
  69.1 1.7 %solid0.1 = (f32[768,128]{1,0:T(8,128)}, f32[128,128]{1,0:T(8,128)S(1)}, f32[8,128]{1,0:T(8,128)S(1)}) custom-call(f32[256,128]{1,0:T(8,128)S(1)} %bitcast.24, f32[8,256]{1,0:T(8,128)S(1)} %copy-done.9, f32[128,128]{1,0:T(8,128)S(1)} %copy-done.5, f32[128,128]{1,0:T(8,128)S(1)} %copy-done.6, f32[128,128]{1,0:T(8,128)S(1)} %copy-done.7, ...), custom_call_target="tpu_custom_call" | custom-call | flops 1000000 | bytes 1000000 | tf_op jit(solution)/shard_map/solid0/pallas_call | solution.py:45
  70.9 9.3 %all-to-all-start.3 = ((f32[128,1,768]{2,1,0:T(1,128)}), f32[128,1,768]{2,1,0:T(1,128)S(1)}, u32[]{:S(2)}, u32[]{:S(2)}) async-start(f32[128,1,768]{2,1,0:T(1,128)} %bitcast.11), calls=%async_computation.3 | async-start | bytes 786432 | tf_op jit(solution)/shard_map/all_to_all | solution.py:455
  80.2 3.5 %collective-permute-start.2 = (f32[96,128]{1,0:T(8,128)}, f32[96,128]{1,0:T(8,128)S(1)}, u32[]{:S(2)}, u32[]{:S(2)}) collective-permute-start(f32[96,128]{1,0:T(8,128)} %get-tuple-element.49), channel_id=1, source_target_pairs={{0,1},{1,2},{2,3},{3,4},{4,5},{5,6},{6,7},{7,8},{8,9},{9,10},{10,1... | collective-permute-start | bytes 147464 | tf_op jit(solution)/shard_map/ppermute | solution.py:462
  83.7 1.9 %collective-permute-start.3 = (f32[96,128]{1,0:T(8,128)}, f32[96,128]{1,0:T(8,128)S(1)}, u32[]{:S(2)}, u32[]{:S(2)}) collective-permute-start(f32[96,128]{1,0:T(8,128)} %get-tuple-element.50), channel_id=1, source_target_pairs={{1,0},{2,1},{3,2},{4,3},{5,4},{6,5},{7,6},{8,7},{9,8},{10,9},{11,1... | collective-permute-start | bytes 147464 | tf_op jit(solution)/shard_map/ppermute | solution.py:462
  85.7 0.1 collective-permute-done.2.left_ref
  85.8 3.9 %collective-permute-done.3.right_ref = f32[96,128]{1,0:T(8,128)S(1)} collective-permute-done((f32[96,128]{1,0:T(8,128)}, f32[96,128]{1,0:T(8,128)S(1)}, u32[]{:S(2)}, u32[]{:S(2)}) %collective-permute-start.3) | collective-permute-done | bytes 49184 | tf_op jit(solution)/shard_map/ppermute | solution.py:462
  89.7 2.6 %all-to-all-done.3 = f32[128,1,768]{2,1,0:T(1,128)S(1)} async-done(((f32[128,1,768]{2,1,0:T(1,128)}), f32[128,1,768]{2,1,0:T(1,128)S(1)}, u32[]{:S(2)}, u32[]{:S(2)}) %all-to-all-start.3) | async-done | bytes 393248 | tf_op jit(solution)/shard_map/all_to_all | solution.py:455
  92.3 0.0 copy-done.12
  92.3 1.0 copy-done.4
  93.2 1.9 %thin1.1 = (f32[256,128]{1,0:T(8,128)}, f32[144,128]{1,0:T(8,128)S(1)}) custom-call(f32[768,128]{1,0:T(8,128)S(1)} %bitcast.22, f32[144,128]{1,0:T(8,128)S(1)} %get-tuple-element.39.poscol_ref, f32[8,128]{1,0:T(8,128)S(1)} %get-tuple-element.40.posrow_ref.after_ref, f32[576,128]{1,0:T(8,128)S(1)} %copy-done.1, f32[576,128]{1,0:T(8,128)S(1)} %copy-done.3, ...), custom_call_target="tpu_custom_call" | custom-call | flops 1000000 | bytes 1000000 | tf_op jit(solution)/shard_map/thin1/pallas_call | solution.py:45
  95.2 0.6 copy-done.15
  95.8 9.2 %all-to-all-start.4 = ((f32[128,2,128]{2,1,0:T(2,128)}), f32[128,2,128]{2,1,0:T(2,128)S(1)}, u32[]{:S(2)}, u32[]{:S(2)}) async-start(f32[128,2,128]{2,1,0:T(2,128)} %bitcast.13), calls=%async_computation.4 | async-start | bytes 262144 | tf_op jit(solution)/shard_map/all_to_all | solution.py:455
  105.0 0.0 copy-done.10
  105.0 0.0 copy-done.11
  105.0 7.6 %full1.1 = (f32[4096,128]{1,0:T(8,128)}, f32[8,128]{1,0:T(8,128)}) custom-call(f32[4224,128]{1,0:T(8,128)} %get-tuple-element.36.b_hbm, f32[4224,128]{1,0:T(8,128)} %get-tuple-element.37.inv_hbm, f32[144,128]{1,0:T(8,128)} %copy-done.15, bf16[128,128]{1,0:T(8,128)(2,1)} %add_convert_fusion.tri_ref, f32[4096,128]{1,0:T(8,128)} %get-tuple-element.52.s_hbm, ...), custom_call_target="tpu_custom_call" | custom-call | flops 4000000000 | bytes 10000000 | tf_op jit(solution)/shard_map/full1/pallas_call | solution.py:45
  112.6 2.4 %all-to-all-done.4 = f32[128,2,128]{2,1,0:T(2,128)S(1)} async-done(((f32[128,2,128]{2,1,0:T(2,128)}), f32[128,2,128]{2,1,0:T(2,128)S(1)}, u32[]{:S(2)}, u32[]{:S(2)}) %all-to-all-start.4) | async-done | bytes 131104 | tf_op jit(solution)/shard_map/all_to_all | solution.py:455
  115.0 0.7 copy-done.14
  115.6 1.2 solid1.1
  116.9 7.4 %all-to-all-start.5 = ((f32[128,1,128]{2,1,0:T(1,128)}), f32[128,1,128]{2,1,0:T(1,128)S(1)}, u32[]{:S(2)}, u32[]{:S(2)}) async-start(f32[128,1,128]{2,1,0:T(1,128)} %bitcast.17), calls=%async_computation.5 | async-start | bytes 131072 | tf_op jit(solution)/shard_map/all_to_all | solution.py:455
  124.3 7.6 %full2.1 = (f32[4096,128]{1,0:T(8,128)}, f32[8,128]{1,0:T(8,128)}) custom-call(f32[4224,128]{1,0:T(8,128)} %get-tuple-element.36.b_hbm, f32[4224,128]{1,0:T(8,128)} %get-tuple-element.37.inv_hbm, f32[144,128]{1,0:T(8,128)} %copy-done.15, bf16[128,128]{1,0:T(8,128)(2,1)} %add_convert_fusion.tri_ref, ...), custom_call_target="tpu_custom_call", output_to_operand_aliasing={{0}: (8, {})} | custom-call | flops 4000000000 | bytes 10000000 | tf_op jit(solution)/shard_map/full2/pallas_call | solution.py:45
  131.8 1.9 %all-to-all-done.5 = f32[128,1,128]{2,1,0:T(1,128)S(1)} async-done(((f32[128,1,128]{2,1,0:T(1,128)}), f32[128,1,128]{2,1,0:T(1,128)S(1)}, u32[]{:S(2)}, u32[]{:S(2)}) %all-to-all-start.5) | async-done | bytes 65568 | tf_op jit(solution)/shard_map/all_to_all | solution.py:455
  133.8 0.5 add_sqrt_fusion
  (18 shorter events, 0.1 us)
Async XLA Ops:
  0.6 8.1 %copy-start.17 = (s32[128,1]{0,1:T(1,128)S(1)}, s32[128,1]{0,1:T(1,128)}, u32[]{:S(2)}) copy-start(s32[128,1]{0,1:T(1,128)} %param.11) | copy-start | bytes 1540
  0.6 8.1 %copy-start.18 = (s32[128,1]{0,1:T(1,128)S(1)}, s32[128,1]{0,1:T(1,128)}, u32[]{:S(2)}) copy-start(s32[128,1]{0,1:T(1,128)} %param.12) | copy-start | bytes 1540
  0.7 28.9 %copy-start.5 = (f32[128,128]{1,0:T(8,128)S(1)}, f32[128,128]{1,0:T(8,128)}, u32[]{:S(2)}) copy-start(f32[128,128]{1,0:T(8,128)} %disp_ref.3) | copy-start | bytes 196612
  0.7 36.5 %copy-start.21 = (f32[16]{0:T(128)S(1)}, f32[16]{0:T(128)}, u32[]{:S(2)}) copy-start(f32[16]{0:T(128)} %param.10) | copy-start | bytes 196
  2.2 35.0 %collective-permute-start = (f32[128,128]{1,0:T(8,128)}, f32[128,128]{1,0:T(8,128)S(1)}, u32[]{:S(2)}, u32[]{:S(2)}) collective-permute-start(f32[128,128]{1,0:T(8,128)} %get-tuple-element.32), channel_id=1, source_target_pairs={{0,1},{1,2},{2,3},{3,4},{4,5},{5,6},{6,7},{7,8},{8,9},{9,10},{10,1... | collective-permute-start | bytes 196616 | tf_op jit(solution)/shard_map/ppermute | solution.py:462
  6.8 30.4 %collective-permute-start.1 = (f32[128,128]{1,0:T(8,128)}, f32[128,128]{1,0:T(8,128)S(1)}, u32[]{:S(2)}, u32[]{:S(2)}) collective-permute-start(f32[128,128]{1,0:T(8,128)} %get-tuple-element.33), channel_id=1, source_target_pairs={{1,0},{2,1},{3,2},{4,3},{5,4},{6,5},{7,6},{8,7},{9,8},{10,9},{11,1... | collective-permute-start | bytes 196616 | tf_op jit(solution)/shard_map/ppermute | solution.py:462
  9.6 82.7 %copy-start.12 = (f32[8,128]{1,0:T(8,128)}, f32[8,128]{1,0:T(8,128)S(1)}, u32[]{:S(2)}) copy-start(f32[8,128]{1,0:T(8,128)S(1)} %get-tuple-element.40.posrow_ref.after_ref) | copy-start | bytes 12292
  9.6 20.0 %all-to-all-start = ((f32[128,1,128]{2,1,0:T(1,128)}), f32[128,1,128]{2,1,0:T(1,128)S(1)}, u32[]{:S(2)}, u32[]{:S(2)}) async-start(f32[128,1,128]{2,1,0:T(1,128)} %bitcast.5), calls=%async_computation | async-start | bytes 131072 | tf_op jit(solution)/shard_map/all_to_all | solution.py:455
  31.3 0.6 copy-start.8
  31.8 16.7 %all-to-all-start.1 = ((f32[128,1,768]{2,1,0:T(1,128)}), f32[128,1,768]{2,1,0:T(1,128)S(1)}, u32[]{:S(2)}, u32[]{:S(2)}) async-start(f32[128,1,768]{2,1,0:T(1,128)} %bitcast.7), calls=%async_computation.1 | async-start | bytes 786432 | tf_op jit(solution)/shard_map/all_to_all | solution.py:455
  37.2 0.6 copy-start.19
  37.2 0.6 copy-start.20
  48.5 1.0 copy-start
  49.5 1.0 copy-start.2
  52.3 0.6 copy-start.16
  53.0 15.5 %all-to-all-start.2 = ((f32[128,2,128]{2,1,0:T(2,128)}), f32[128,2,128]{2,1,0:T(2,128)S(1)}, u32[]{:S(2)}, u32[]{:S(2)}) async-start(f32[128,2,128]{2,1,0:T(2,128)} %bitcast.9), calls=%async_computation.2 | async-start | bytes 262144 | tf_op jit(solution)/shard_map/all_to_all | solution.py:455
  58.5 9.9 %copy-start.6 = (f32[128,128]{1,0:T(8,128)S(1)}, f32[128,128]{1,0:T(8,128)}, u32[]{:S(2)}) copy-start(f32[128,128]{1,0:T(8,128)} %load_ref.3) | copy-start | bytes 196612
  58.5 9.9 %copy-start.7 = (f32[128,128]{1,0:T(8,128)S(1)}, f32[128,128]{1,0:T(8,128)}, u32[]{:S(2)}) copy-start(f32[128,128]{1,0:T(8,128)} %comp_ref.3) | copy-start | bytes 196612
  58.5 9.9 %copy-start.9 = (f32[8,256]{1,0:T(8,128)S(1)}, f32[8,256]{1,0:T(8,128)}, u32[]{:S(2)}) copy-start(f32[8,256]{1,0:T(8,128)} %copy-done.8) | copy-start | bytes 24580
  58.5 33.7 %copy-start.1 = (f32[576,128]{1,0:T(8,128)S(1)}, f32[576,128]{1,0:T(8,128)}, u32[]{:S(2)}) copy-start(f32[576,128]{1,0:T(8,128)} %get-tuple-element.41.bt_ref) | copy-start | bytes 884740
  58.5 33.7 %copy-start.3 = (f32[576,128]{1,0:T(8,128)S(1)}, f32[576,128]{1,0:T(8,128)}, u32[]{:S(2)}) copy-start(f32[576,128]{1,0:T(8,128)} %get-tuple-element.42.it_ref) | copy-start | bytes 884740
  68.4 0.7 copy-start.13
  70.9 21.4 %all-to-all-start.3 = ((f32[128,1,768]{2,1,0:T(1,128)}), f32[128,1,768]{2,1,0:T(1,128)S(1)}, u32[]{:S(2)}, u32[]{:S(2)}) async-start(f32[128,1,768]{2,1,0:T(1,128)} %bitcast.11), calls=%async_computation.3 | async-start | bytes 786432 | tf_op jit(solution)/shard_map/all_to_all | solution.py:455
  80.2 5.6 %collective-permute-start.2 = (f32[96,128]{1,0:T(8,128)}, f32[96,128]{1,0:T(8,128)S(1)}, u32[]{:S(2)}, u32[]{:S(2)}) collective-permute-start(f32[96,128]{1,0:T(8,128)} %get-tuple-element.49), channel_id=1, source_target_pairs={{0,1},{1,2},{2,3},{3,4},{4,5},{5,6},{6,7},{7,8},{8,9},{9,10},{10,1... | collective-permute-start | bytes 147464 | tf_op jit(solution)/shard_map/ppermute | solution.py:462
  83.7 5.9 %collective-permute-start.3 = (f32[96,128]{1,0:T(8,128)}, f32[96,128]{1,0:T(8,128)S(1)}, u32[]{:S(2)}, u32[]{:S(2)}) collective-permute-start(f32[96,128]{1,0:T(8,128)} %get-tuple-element.50), channel_id=1, source_target_pairs={{1,0},{2,1},{3,2},{4,3},{5,4},{6,5},{7,6},{8,7},{9,8},{10,9},{11,1... | collective-permute-start | bytes 147464 | tf_op jit(solution)/shard_map/ppermute | solution.py:462
  85.8 19.2 %copy-start.10 = (f32[96,128]{1,0:T(8,128)}, f32[96,128]{1,0:T(8,128)S(1)}, u32[]{:S(2)}) copy-start(f32[96,128]{1,0:T(8,128)S(1)} %collective-permute-done.2.left_ref) | copy-start | bytes 147460
  89.7 15.4 %copy-start.11 = (f32[96,128]{1,0:T(8,128)}, f32[96,128]{1,0:T(8,128)S(1)}, u32[]{:S(2)}) copy-start(f32[96,128]{1,0:T(8,128)S(1)} %collective-permute-done.3.right_ref) | copy-start | bytes 147460
  92.3 1.0 copy-start.4
  95.2 0.6 copy-start.15
  95.8 19.2 %all-to-all-start.4 = ((f32[128,2,128]{2,1,0:T(2,128)}), f32[128,2,128]{2,1,0:T(2,128)S(1)}, u32[]{:S(2)}, u32[]{:S(2)}) async-start(f32[128,2,128]{2,1,0:T(2,128)} %bitcast.13), calls=%async_computation.4 | async-start | bytes 262144 | tf_op jit(solution)/shard_map/all_to_all | solution.py:455
  115.0 0.7 copy-start.14
  116.9 16.9 %all-to-all-start.5 = ((f32[128,1,128]{2,1,0:T(1,128)}), f32[128,1,128]{2,1,0:T(1,128)S(1)}, u32[]{:S(2)}, u32[]{:S(2)}) async-start(f32[128,1,128]{2,1,0:T(1,128)} %bitcast.17), calls=%async_computation.5 | async-start | bytes 131072 | tf_op jit(solution)/shard_map/all_to_all | solution.py:455
